TPU v7x, 32 devices: a whole 2x2x4 slice. The times are simulated.
32 devices in a mesh: shot: 4 (over y, core), gx: 4 (over z), gy: 2 (over x).
Axes of the slice: x: 2, y: 2, z: 4, core: 2. Of those that a mesh axis runs over, the one named last changes fastest.
Arguments:
- latent: float32 [32, 24, 1024], P('shot', 'gx', 'gy'), may hold values from -6 to 6
- w_first: float32 [64, 64], replicated, may hold values from -0.75 to 0.75
- w_second: float32 [64, 128], replicated, may hold values from -0.75 to 0.75
- fwd_press: float32 [4, 96, 64, 128], P('shot', 'gx', 'gy'), may hold values from -1.5 to 8
- fwd_vel: float32 [4, 3, 96, 64, 128], P('shot', None, 'gx', 'gy'), may hold values from -1.5 to 8
- adj_press: float32 [4, 96, 64, 128], P('shot', 'gx', 'gy'), may hold values from -1.5 to 8
- adj_vel: float32 [4, 3, 96, 64, 128], P('shot', None, 'gx', 'gy'), may hold values from -1.5 to 8
- src_pos: int32 [3, 4], P(None, 'shot'), may hold values from 0 to 127, as said below
- src_amp: float32 [3, 4], P(None, 'shot'), may hold values from -24 to 24
- rec_pos: int32 [4, 3, 2048], P('shot'), may hold values from 0 to 127, as said below
- observed: float32 [4, 3, 2048], P('shot'), may hold values from -6 to 6
Outputs:
- grad_latent: float32 [32, 24, 1024], P('shot', 'gx', 'gy')
- grad_first: float32 [64, 64], replicated
- grad_second: float32 [64, 128], replicated
Inputs may be any that keep to these rules, and one draw needn't show every extreme that they name: `src_pos`: row 0 is an x cell below 96, row 1 a y cell below 64, row 2 a depth cell below 128. `rec_pos`: component 0 is an x cell below 96, component 1 a y cell below 64, component 2 a depth cell below 128; cells may repeat.
All inputs are finite; a program needn't handle non-finite values.
Results may differ from a plain program's by a relative error of at most 0.0003.
Values sent between devices are 32-bit elements; how exact they have to be, the bound alone decides.
A program may use at most 64 MiB of HBM per device.

v0:
```python
import jax
import jax.numpy as jnp
from jax import lax
from jax.experimental import pallas as pl
from jax.experimental.pallas import tpu as pltpu
from jax.sharding import PartitionSpec as P

CH = 64
STEPS = 3


coeffs = (1225.0 / 1024.0, -245.0 / 3072.0, 49.0 / 5120.0, -5.0 / 7168.0)


def decode(latent, w_first, w_second):
    depth_c, rows_x, merged = latent.shape
    rows_y = merged // CH
    flattened = latent.reshape(-1, CH)
    hidden = jnp.tanh(jnp.dot(flattened, w_first, precision=lax.Precision.HIGHEST))
    outputs = jnp.dot(hidden, w_second, precision=lax.Precision.HIGHEST)
    fine_out = (
        outputs.reshape(depth_c, rows_x, rows_y, 2, 4, 4, 4)
        .transpose(3, 1, 4, 2, 5, 0, 6)
        .reshape(2, rows_x * 4, rows_y * 4, depth_c * 4)
    )
    return (flattened, hidden, fine_out)


def materials(fine_out):
    wave_speed = 0.15 + 0.25 * jax.nn.sigmoid(fine_out[0])
    density = 1.0 + 1.5 * jax.nn.sigmoid(fine_out[1])
    return (density * wave_speed * wave_speed, 1.0 / density)


def decoder_grads(flattened, hidden, fine_out, grad_mod, grad_buoy, w_first, w_second):
    sig_speed = jax.nn.sigmoid(fine_out[0])
    sig_dens = jax.nn.sigmoid(fine_out[1])
    wave_speed = 0.15 + 0.25 * sig_speed
    density = 1.0 + 1.5 * sig_dens
    grad_speed = grad_mod * 2.0 * density * wave_speed
    grad_dens = grad_mod * wave_speed * wave_speed - grad_buoy / (density * density)
    grad_fine = jnp.stack(
        [
            grad_speed * 0.25 * sig_speed * (1.0 - sig_speed),
            grad_dens * 1.5 * sig_dens * (1.0 - sig_dens),
        ]
    )
    size_x, size_y, size_z = (grad_fine.shape[1], grad_fine.shape[2], grad_fine.shape[3])
    grad_out = (
        grad_fine.reshape(2, size_x // 4, 4, size_y // 4, 4, size_z // 4, 4)
        .transpose(5, 1, 3, 0, 2, 4, 6)
        .reshape(-1, 128)
    )
    grad_hidden = jnp.dot(grad_out, w_second.T, precision=lax.Precision.HIGHEST)
    grad_pre = grad_hidden * (1.0 - hidden * hidden)
    grad_latent = jnp.dot(grad_pre, w_first.T, precision=lax.Precision.HIGHEST).reshape(
        size_z // 4, size_x // 4, size_y // 4 * CH
    )
    grad_second = jnp.dot(hidden.T, grad_out, precision=lax.Precision.HIGHEST)
    grad_first = jnp.dot(flattened.T, grad_pre, precision=lax.Precision.HIGHEST)
    return (grad_latent, grad_first, grad_second)


RIM = 7
VRIM = 4
PAD = 8


def receiver_kernel(column_ref, depth_ref, parts_ref, hits_ref, recorded_ref, weights_ref):
    count = column_ref.shape[1]
    size_x, size_y, size_z = hits_ref.shape
    deep = (
        lax.broadcasted_iota(jnp.int32, (size_z, count), 0) == depth_ref[...]
    ).astype(jnp.float32)
    weights_ref[pl.ds(0, size_z), :] = deep.astype(jnp.bfloat16)
    for part in range(2 * STEPS):
        weights_ref[pl.ds((part + 1) * size_z, size_z), :] = (
            deep * parts_ref[pl.ds(part, 1), :]
        ).astype(jnp.bfloat16)
    chunk = 8 if size_x % 8 == 0 else 1
    rows = chunk * size_y

    def planes(step, carry):
        index = lax.broadcasted_iota(jnp.int32, (rows, count), 0) + step * rows
        picks = (index == column_ref[...]).astype(jnp.float32).astype(jnp.bfloat16)
        summed = lax.dot_general(
            picks, weights_ref[...], (((1,), (1,)), ((), ())), preferred_element_type=jnp.float32
        ).reshape(chunk, size_y, (2 * STEPS + 1) * size_z)
        here = pl.ds(step * chunk, chunk)
        hits_ref[here] = summed[:, :, :size_z]
        for moment in range(STEPS):
            first = (1 + 2 * moment) * size_z
            recorded_ref[moment, here] = (
                summed[:, :, first : first + size_z]
                + summed[:, :, first + size_z : first + 2 * size_z]
            )
        return carry

    lax.fori_loop(0, size_x // chunk, planes, 0)


def receiver_fields(receivers, observed_now, anchor_x, anchor_y, shape):
    size_x, size_y, size_z = shape
    local_x = receivers[0] - anchor_x
    local_y = receivers[1] - anchor_y
    inside = (local_x >= 0) & (local_x < size_x) & (local_y >= 0) & (local_y < size_y)
    column = jnp.where(inside, local_x * size_y + local_y, -1)
    count = column.shape[0]
    high = lax.reduce_precision(observed_now, 8, 7)
    low = lax.reduce_precision(observed_now - high, 8, 7)
    parts = jnp.stack([high, low], axis=1).reshape(2 * STEPS, count)
    return pl.pallas_call(
        receiver_kernel,
        out_shape=(
            jax.ShapeDtypeStruct(shape, jnp.float32),
            jax.ShapeDtypeStruct((STEPS,) + shape, jnp.float32),
        ),
        scratch_shapes=[pltpu.VMEM(((2 * STEPS + 1) * size_z, count), jnp.bfloat16)],
        compiler_params=pltpu.CompilerParams(vmem_limit_bytes=40 * 1024 * 1024),
        cost_estimate=pl.CostEstimate(
            flops=2 * size_x * size_y * count * 7 * size_z,
            bytes_accessed=16 * size_x * size_y * size_z,
            transcendentals=0,
        ),
    )(column[None, :], receivers[2][None, :], parts)


def window_kernel(
    place_ref,
    amp_ref,
    dplus_ref,
    dminus_ref,
    mod_ref,
    buoy_ref,
    fwd_press,
    fwd_vel,
    adj_press,
    adj_vel,
    hits_ref,
    recorded_ref,
    out_ref,
    press,
    buoy,
    vel_x,
    vel_y,
    vel_z,
    diverge_z,
    misfit,
    div_at,
    slope_x,
    slope_y,
    slope_z,
    local_sem,
    send_sem,
    recv_sem,
):
    size_x, size_y, size_z = mod_ref.shape
    tall = size_y + 2 * PAD
    mid_y = pl.ds(PAD, size_y)
    me_x, me_y = lax.axis_index("gx"), lax.axis_index("gy")
    has = (
        me_x > 0,
        me_x < lax.axis_size("gx") - 1,
        me_y > 0,
        me_y < lax.axis_size("gy") - 1,
    )
    target = ({"gx": me_x - 1}, {"gx": me_x + 1}, {"gy": me_y - 1}, {"gy": me_y + 1})

    barrier = pltpu.get_barrier_semaphore()
    for side in range(4):

        @pl.when(has[side])
        def _():
            pl.semaphore_signal(
                barrier, inc=1, device_id=target[side], device_id_type=pl.DeviceIdType.MESH
            )

    loads = [
        (fwd_press, press.at[0, pl.ds(RIM, size_x), mid_y]),
        (buoy_ref, buoy.at[pl.ds(VRIM, size_x), mid_y]),
    ]
    for way, vel in enumerate((fwd_vel, adj_vel)):
        loads.append((vel.at[0], vel_x.at[way, pl.ds(VRIM, size_x)]))
        loads.append((vel.at[1], vel_y.at[way, :, mid_y]))
        loads.append((vel.at[2], vel_z.at[way]))
    moves = [
        pltpu.make_async_copy(source, dest, local_sem.at[n])
        for n, (source, dest) in enumerate(loads)
    ]
    for move in moves:
        move.start()

    def channel(slot, pairs):
        return [
            pltpu.make_async_remote_copy(
                src_ref=pairs[side][0],
                dst_ref=pairs[side][1],
                send_sem=send_sem.at[slot, side],
                recv_sem=recv_sem.at[slot, side ^ 1],
                device_id=target[side],
                device_id_type=pl.DeviceIdType.MESH,
            )
            for side in range(4)
        ]

    def press_pairs(state, edges):
        low_x, high_x = pl.ds(0, RIM), pl.ds(size_x + RIM, RIM)
        low_y, high_y = pl.ds(0, PAD), pl.ds(size_y + PAD, PAD)
        mid_x = pl.ds(RIM, size_x)
        return [
            (edges[0], press.at[state, high_x, mid_y]),
            (edges[1], press.at[state, low_x, mid_y]),
            (edges[2], press.at[state, mid_x, high_y]),
            (edges[3], press.at[state, mid_x, low_y]),
        ]

    def own_edges(state):
        mid_x = pl.ds(RIM, size_x)
        return [
            press.at[state, pl.ds(RIM, RIM), mid_y],
            press.at[state, pl.ds(size_x, RIM), mid_y],
            press.at[state, mid_x, pl.ds(PAD, PAD)],
            press.at[state, mid_x, pl.ds(size_y, PAD)],
        ]

    first_edges = [
        fwd_press.at[pl.ds(0, RIM)],
        fwd_press.at[pl.ds(size_x - RIM, RIM)],
        fwd_press.at[:, pl.ds(0, PAD)],
        fwd_press.at[:, pl.ds(size_y - PAD, PAD)],
    ]
    channels = [channel(0, press_pairs(0, first_edges))]
    for state in range(1, 2 * STEPS):
        channels.append(channel(state, press_pairs(state, own_edges(state))))
    for way, vel in enumerate((fwd_vel, adj_vel)):
        channels.append(
            channel(
                2 * STEPS + way,
                [
                    (vel.at[0, pl.ds(0, VRIM)], vel_x.at[way, pl.ds(size_x + VRIM, VRIM)]),
                    (vel.at[0, pl.ds(size_x - VRIM, VRIM)], vel_x.at[way, pl.ds(0, VRIM)]),
                    (vel.at[1, :, pl.ds(0, PAD)], vel_y.at[way, :, pl.ds(size_y + PAD, PAD)]),
                    (vel.at[1, :, pl.ds(size_y - PAD, PAD)], vel_y.at[way, :, pl.ds(0, PAD)]),
                ],
            )
        )
    mid_v = pl.ds(VRIM, size_x)
    channels.append(
        channel(
            2 * STEPS + 2,
            [
                (buoy_ref.at[pl.ds(0, VRIM)], buoy.at[pl.ds(size_x + VRIM, VRIM), mid_y]),
                (buoy_ref.at[pl.ds(size_x - VRIM, VRIM)], buoy.at[pl.ds(0, VRIM), mid_y]),
                (buoy_ref.at[:, pl.ds(0, PAD)], buoy.at[mid_v, pl.ds(size_y + PAD, PAD)]),
                (buoy_ref.at[:, pl.ds(size_y - PAD, PAD)], buoy.at[mid_v, pl.ds(0, PAD)]),
            ],
        )
    )

    def send(slot, sides):
        for side in sides:

            @pl.when(has[side])
            def _():
                channels[slot][side].start()

    def receive(slot):
        for side in range(4):

            @pl.when(has[side])
            def _():
                channels[slot][side ^ 1].wait_recv()

    def sent(slot):
        for side in range(4):

            @pl.when(has[side])
            def _():
                channels[slot][side].wait_send()

    for side in range(4):

        @pl.when(jnp.logical_not(has[side]))
        def _():
            far = side % 2
            if side < 2:
                rows = pl.ds(far * (size_x + RIM), RIM)
                vrows = pl.ds(far * (size_x + VRIM), VRIM)
                for state in range(2 * STEPS):
                    press[state, rows, mid_y] = jnp.zeros((RIM, size_y, size_z), jnp.float32)
                buoy[vrows, mid_y] = jnp.zeros((VRIM, size_y, size_z), jnp.float32)
                for way in range(2):
                    vel_x[way, vrows] = jnp.zeros((VRIM, size_y, size_z), jnp.float32)
            else:
                cols = pl.ds(far * (size_y + PAD), PAD)
                blank = jnp.zeros((size_x, PAD, size_z), jnp.float32)
                for state in range(2 * STEPS):
                    press[state, pl.ds(RIM, size_x), cols] = blank
                buoy[mid_v, cols] = blank
                for way in range(2):
                    vel_y[way, :, cols] = blank

    peers = sum(jnp.where(here, 1, 0) for here in has)
    pl.semaphore_wait(barrier, peers)

    every = range(4)
    send(0, every)
    send(2 * STEPS + 2, every)
    send(2 * STEPS, every)
    send(2 * STEPS + 1, every)
    for move in moves:
        move.wait()

    src_x, src_y, src_z = place_ref[0], place_ref[1], place_ref[2]
    at_source = (
        (lax.broadcasted_iota(jnp.int32, (size_y, size_z), 0) == src_y)
        & (lax.broadcasted_iota(jnp.int32, (size_y, size_z), 1) == src_z)
    ).astype(jnp.float32)
    chunk = 8 if size_x % 8 == 0 else 1
    exact = lax.Precision.HIGHEST

    def step(state, way, moment):
        def depth_part(turn, carry):
            here = pl.ds(turn * chunk, chunk)
            inner = press[state, pl.ds(turn * chunk + RIM, chunk), mid_y]
            slope = jnp.dot(
                inner.reshape(chunk * size_y, size_z), dplus_ref[...], precision=exact
            ).reshape(inner.shape)
            if way == 0:
                slope_z[moment, here] = slope
            moved = vel_z[way, here] - buoy_ref_in(turn) * slope
            vel_z[way, here] = moved
            diverge_z[here] = jnp.dot(
                moved.reshape(chunk * size_y, size_z), dminus_ref[...], precision=exact
            ).reshape(inner.shape)
            return carry

        def buoy_ref_in(turn):
            return buoy[pl.ds(turn * chunk + VRIM, chunk), mid_y]

        lax.fori_loop(0, size_x // chunk, depth_part, 0)

        if state == 0:
            receive(2 * STEPS + 2)
        if state % STEPS == 0:
            receive(2 * STEPS + way)
        receive(state)

        def along_x(i):
            slope = 0.0
            for order, weight in enumerate(coeffs):
                r = order + 1
                slope = slope + weight * (
                    press[state, i + VRIM - 1 + r, mid_y] - press[state, i + VRIM - r, mid_y]
                )
            vel_x[way, i] = vel_x[way, i] - buoy[i, mid_y] * slope
            return slope

        def ghost_low(i, carry):
            along_x(i)
            return carry

        def faces(x, carry):
            slope = along_x(x + VRIM)
            plane = press[state, x + RIM]
            slope_b = 0.0
            for order, weight in enumerate(coeffs):
                r = order + 1
                back = plane if r == 1 else pltpu.roll(plane, r - 1, 0)
                slope_b = slope_b + weight * (pltpu.roll(plane, tall - r, 0) - back)
            vel_y[way, x] = vel_y[way, x] - buoy[x + VRIM] * slope_b
            if way == 0:
                slope_x[moment, x] = slope
                slope_y[moment, x] = slope_b[PAD : PAD + size_y]
            return carry

        lax.fori_loop(0, VRIM, ghost_low, 0)
        lax.fori_loop(size_x + VRIM, size_x + 2 * VRIM - 1, ghost_low, 0)
        lax.fori_loop(0, size_x, faces, 0)

        def finish(k, carry):
            x = lax.rem(k + size_x - RIM, size_x)
            plane = vel_y[way, x]
            div = diverge_z[x]
            across = 0.0
            for order, weight in enumerate(coeffs):
                r = order + 1
                ahead = plane if r == 1 else pltpu.roll(plane, tall - r + 1, 0)
                across = across + weight * (ahead - pltpu.roll(plane, r, 0))
                div = div + weight * (
                    vel_x[way, x + VRIM + r - 1] - vel_x[way, x + VRIM - r]
                )
            div = div + across[PAD : PAD + size_y]
            value = press[state, x + RIM, mid_y] - mod_ref[x] * div
            if way == 0:
                value = value + at_source * jnp.where(x == src_x, amp_ref[moment], 0.0)
                residue = hits_ref[x] * value - recorded_ref[moment, x]
                div_at[moment, x] = div
                if moment == STEPS - 1:
                    press[state + 1, x + RIM, mid_y] = adj_press[x] + residue
                else:
                    misfit[moment, x] = residue
                    press[state + 1, x + RIM, mid_y] = value
            else:
                part_mod = value * div_at[moment, x]
                part_buoy = (
                    vel_x[way, x + VRIM] * slope_x[moment, x]
                    + plane[PAD : PAD + size_y] * slope_y[moment, x]
                    + vel_z[way, x] * slope_z[moment, x]
                )
                if moment == STEPS - 1:
                    out_ref[0, x] = -part_mod
                    out_ref[1, x] = -part_buoy
                else:
                    out_ref[0, x] = out_ref[0, x] - part_mod
                    out_ref[1, x] = out_ref[1, x] - part_buoy
                if moment > 0:
                    press[state + 1, x + RIM, mid_y] = value + misfit[moment - 1, x]
            return carry

        edge = min(2 * RIM, size_x)
        lax.fori_loop(0, edge, finish, 0)
        more = state + 1 < 2 * STEPS
        if more:
            send(state + 1, (0, 1))
        lax.fori_loop(edge, size_x, finish, 0)
        if more:
            send(state + 1, (2, 3))

    for moment in range(STEPS):
        step(moment, 0, moment)
    for turn in range(STEPS):
        step(STEPS + turn, 1, STEPS - 1 - turn)
    for slot in range(2 * STEPS + 3):
        sent(slot)


def depth_matrices(size_z):
    source = lax.broadcasted_iota(jnp.int32, (size_z, size_z), 0)
    dest = lax.broadcasted_iota(jnp.int32, (size_z, size_z), 1)
    plus = jnp.zeros((size_z, size_z), jnp.float32)
    minus = plus
    for order, weight in enumerate(coeffs):
        r = order + 1
        plus = plus + jnp.where(source == dest + r, weight, 0.0)
        plus = plus - jnp.where(source == dest - r + 1, weight, 0.0)
        minus = minus + jnp.where(source == dest + r - 1, weight, 0.0)
        minus = minus - jnp.where(source == dest - r, weight, 0.0)
    return plus, minus


def window(place, amps, modulus, buoyancy, fwd_press, fwd_vel, adj_press, adj_vel, hits, recorded):
    size_x, size_y, size_z = fwd_press.shape
    tall = size_y + 2 * PAD
    plus, minus = depth_matrices(size_z)
    vmem = pl.BlockSpec(memory_space=pltpu.VMEM)
    smem = pl.BlockSpec(memory_space=pltpu.SMEM)
    field = (size_x, size_y, size_z)

    def scratch(*shape):
        return pltpu.VMEM(shape, jnp.float32)

    slots = 2 * STEPS + 3
    return pl.pallas_call(
        window_kernel,
        out_shape=jax.ShapeDtypeStruct((2,) + field, jnp.float32),
        in_specs=[smem, smem] + [vmem] * 10,
        out_specs=vmem,
        scratch_shapes=[
            scratch(2 * STEPS, size_x + 2 * RIM, tall, size_z),
            scratch(size_x + 2 * VRIM, tall, size_z),
            scratch(2, size_x + 2 * VRIM, size_y, size_z),
            scratch(2, size_x, tall, size_z),
            scratch(2, *field),
            scratch(*field),
            scratch(STEPS - 1, *field),
            scratch(STEPS, *field),
            scratch(STEPS, *field),
            scratch(STEPS, *field),
            scratch(STEPS, *field),
            pltpu.SemaphoreType.DMA((8,)),
            pltpu.SemaphoreType.DMA((slots, 4)),
            pltpu.SemaphoreType.DMA((slots, 4)),
        ],
        compiler_params=pltpu.CompilerParams(
            collective_id=0, has_side_effects=True, vmem_limit_bytes=56 * 1024 * 1024
        ),
    )(place, amps, plus, minus, modulus, buoyancy, fwd_press, fwd_vel, adj_press, adj_vel, hits, recorded)


def body(
    latent,
    w_first,
    w_second,
    fwd_press,
    fwd_vel,
    adj_press,
    adj_vel,
    src_pos,
    src_amp,
    rec_pos,
    observed,
):
    size_x, size_y = (fwd_press.shape[1], fwd_press.shape[2])
    anchor_x = lax.axis_index("gx") * size_x
    anchor_y = lax.axis_index("gy") * size_y
    flattened, hidden, fine_out = decode(latent, w_first, w_second)
    slab_mod, slab_buoy = materials(fine_out)
    stacked = lax.all_gather(jnp.stack([slab_mod, slab_buoy]), "shot", axis=3, tiled=True)
    modulus, buoyancy = (stacked[0], stacked[1])
    hits, recorded = receiver_fields(
        rec_pos[0], observed[0], anchor_x, anchor_y, fwd_press.shape[1:]
    )
    place = jnp.stack([src_pos[0, 0] - anchor_x, src_pos[1, 0] - anchor_y, src_pos[2, 0]])
    totals = window(
        place,
        src_amp[:, 0],
        modulus,
        buoyancy,
        fwd_press[0],
        fwd_vel[0],
        adj_press[0],
        adj_vel[0],
        hits,
        recorded,
    )
    shares = lax.psum_scatter(totals, "shot", scatter_dimension=3, tiled=True)
    grad_latent, grad_first, grad_second = decoder_grads(
        flattened, hidden, fine_out, shares[0], shares[1], w_first, w_second
    )
    grad_first, grad_second = lax.psum((grad_first, grad_second), ("shot", "gx", "gy"))
    return (grad_latent, grad_first, grad_second)


def solution(mesh):
    in_specs = (
        P("shot", "gx", "gy"),
        P(),
        P(),
        P("shot", "gx", "gy", None),
        P("shot", None, "gx", "gy", None),
        P("shot", "gx", "gy", None),
        P("shot", None, "gx", "gy", None),
        P(None, "shot"),
        P(None, "shot"),
        P("shot", None, None),
        P("shot", None, None),
    )
    out_specs = (P("shot", "gx", "gy"), P(), P())
    return jax.shard_map(body, mesh=mesh, in_specs=in_specs, out_specs=out_specs, check_vma=False)
```

profile of v0, /device:TPU:0, one launch (start us, length us, event | category | flops | bytes accessed | tf_op | source)
XLA Modules:
  0.0 232.9 jit_solution(6990390572586204841)
XLA Ops:
  9.5 1.4 fusion.39
  12.1 0.8 slice_bitcast_fusion
  12.9 0.8 bitcast_reduce-precision_fusion
  13.8 1.0 copy.35
  14.8 1.2 convolution_tanh_fusion
  16.4 3.1 %reshape.237 = f32[8,6,8,2,4,4,4]{2,1,0,6,5,4,3:T(8,128)} reshape(f32[384,128]{0,1:T(8,128)S(1)} %fusion.40) | data formatting | bytes 393216 | tf_op jit(solution)/shard_map/reshape | solution.py:22
  19.5 3.4 %copy.37 = f32[8,6,8,2,4,4,4]{0,2,6,5,4,1,3:T(8,128)S(1)} copy(f32[8,6,8,2,4,4,4]{2,1,0,6,5,4,3:T(8,128)} %reshape.237) | data formatting | bytes 393216 | tf_op jit(solution)/shard_map/reshape | solution.py:22
  22.9 2.5 %fusion.2 = (f32[1,6,4,8,4,8,4]{5,3,6,4,2,1,0:T(8,128)}, f32[1,6,4,8,4,8,4]{5,3,6,4,2,1,0:T(8,128)}) fusion(f32[2,6,4,8,4,8,4]{5,3,6,4,2,1,0:T(8,128)S(1)} %bitcast.56), kind=kLoop, calls=%fused_computation.4 | loop fusion | flops 147456 | bytes 393216 | tf_op jit(solution)/shard_map/div | solution.py:30
  25.4 5.7 %copy.39 = f32[1,6,4,8,4,8,4]{6,5,4,3,2,1,0:T(8,128)S(1)} copy(f32[1,6,4,8,4,8,4]{5,3,6,4,2,1,0:T(8,128)} %get-tuple-element.23) | data formatting | bytes 196608 | tf_op jit(solution)/shard_map/div | solution.py:30
  31.1 1.6 div.74
  32.6 5.7 %copy.38 = f32[1,6,4,8,4,8,4]{6,5,4,3,2,1,0:T(8,128)S(1)} copy(f32[1,6,4,8,4,8,4]{5,3,6,4,2,1,0:T(8,128)} %get-tuple-element.24) | data formatting | bytes 196608 | tf_op jit(solution)/shard_map/div | solution.py:30
  38.4 1.6 div.72
  39.9 1.2 multiply_multiply_fusion.1
  41.6 22.9 %all_gather.3 = f32[2,24,32,128]{2,1,0,3:T(8,128)S(1)} all-gather(f32[2,24,32,32]{2,1,0,3:T(8,128)S(1)} %copy.40), channel_id=1, replica_groups=mesh['shot'=4,'gx'=4,'gy'=2] {'shot'}, dimensions={3}, use_global_device_ids=true | all-gather | bytes 983040 | tf_op jit(solution)/shard_map/all_gather | solution.py:509
  64.8 1.2 copy.52
  66.0 1.2 copy.51
  67.2 1.2 pad_add_fusion.place_ref
  68.5 4.3 %shard_map.130 = (f32[24,32,128]{2,1,0:T(8,128)S(1)}, f32[3,24,32,128]{3,2,1,0:T(8,128)S(1)}) custom-call(s32[1,2048]{1,0:T(1,128)S(1)} %get-tuple-element.34.column_ref, s32[1,2048]{1,0:T(1,128)S(1)} %get-tuple-element.33.depth_ref, f32[6,2048]{1,0:T(8,128)S(1)} %reshape.238.parts_ref), custom_call_target="tpu_custom_call" | custom-call | flops 2818572288 | bytes 1572864 | tf_op jit(solution)/shard_map/pallas_call | solution.py:112
  72.8 1.0 copy-done.1
  73.8 0.7 copy-done.2
  75.4 46.2 %shard_map.131 = f32[2,24,32,128]{3,2,1,0:T(8,128)} custom-call(s32[3]{0:T(128)} %pad_add_fusion.place_ref, f32[3]{0:T(128)} %bitcast.65, f32[128,128]{1,0:T(8,128)} %get-tuple-element.36.dplus_ref, f32[128,128]{1,0:T(8,128)} %get-tuple-element.35.dminus_ref, f32[24,32,128]{2,1,0:T(8,128)} %bitcast.60, f32[24,32,128]{2,1,0:T(8,128)} %bitcast.59, ...), custom_call_target="tpu_custom_call" | custom-call | tf_op jit(solution)/shard_map/pallas_call | solution.py:464
  121.6 2.1 copy.49
  123.7 2.1 reshape.244
  125.8 22.8 %reduce-scatter.4.cloned.1.call-done = f32[32,1536]{1,0:T(8,128)} async-done(((f32[128,1536]{1,0:T(8,128)}), f32[32,1536]{1,0:T(8,128)}) %reduce-scatter.4.cloned.1.call-update) | async-done | bytes 196624
  148.6 1.1 reshape.245
  150.9 1.2 subtract_multiply_fusion
  152.1 1.9 stack.33
  154.0 3.2 %stack.34 = f32[1,6,4,8,4,8,4]{6,5,4,3,2,1,0:T(8,128)} reshape(f32[1,24,32,32]{3,2,1,0:T(8,128)} %get-tuple-element.26) | data formatting | bytes 196608 | tf_op jit(solution)/shard_map/stack | solution.py:42
  157.2 5.7 %maximum_bitcast_fusion = f32[8,6,8,2,4,4,4]{6,0,5,2,4,1,3:T(8,128)} fusion(f32[1,6,4,8,4,8,4]{6,5,4,3,2,1,0:T(8,128)} %stack.34, f32[1,6,4,8,4,8,4]{6,5,4,3,2,1,0:T(8,128)S(1)} %stack.33), kind=kLoop, calls=%fused_computation | loop fusion | flops 49152 | bytes 393216 | tf_op jit(solution)/shard_map/transpose | solution.py:51
  162.9 17.0 %copy.43 = f32[8,6,8,2,4,4,4]{2,1,0,6,5,4,3:T(8,128)} copy(f32[8,6,8,2,4,4,4]{6,0,5,2,4,1,3:T(8,128)} %maximum_bitcast_fusion) | data formatting | bytes 393216 | tf_op jit(solution)/shard_map/transpose | solution.py:51
  179.9 3.0 %reshape.239 = f32[384,128]{0,1:T(8,128)S(1)} reshape(f32[8,6,8,2,4,4,4]{2,1,0,6,5,4,3:T(8,128)} %copy.43) | data formatting | bytes 393216 | tf_op jit(solution)/shard_map/reshape | solution.py:52
  184.3 40.3 %all-reduce = (f32[64,64]{0,1:T(8,128)S(1)}, f32[64,128]{1,0:T(8,128)}) all-reduce(f32[64,64]{0,1:T(8,128)S(1)} %convolution_bitcast_fusion, f32[64,128]{1,0:T(8,128)S(1)} %fusion.42), channel_id=1, replica_groups=mesh['shot'=4,'gx'=4,'gy'=2] {'shot','gx','gy'}, use_global_device_ids=true, to_apply=%region_1.2 | all-reduce | flops 12288 | bytes 98304 | tf_op jit(solution)/shard_map/psum | solution.py:531
  (50 shorter events, 8.3 us)
Async XLA Ops:
  7.2 8.8 %copy-start = (f32[64,128]{1,0:T(8,128)S(1)}, f32[64,128]{1,0:T(8,128)}, u32[]{:S(2)}) copy-start(f32[64,128]{1,0:T(8,128)} %param.13) | copy-start | bytes 98308
  7.2 141.5 %reduce-scatter.4.cloned.1.call-start = ((), (), s32[]{:S(2)}) async-start(), calls=%async_computation.1 | async-start | bytes 983040
  68.4 6.2 %copy-start.6 = (s32[128]{0:T(128)S(1)}, s32[128]{0:T(128)}, u32[]{:S(2)}) copy-start(s32[128]{0:T(128)} %get-tuple-element.46) | copy-start | bytes 1540
  68.4 6.2 %copy-start.7 = (s32[128]{0:T(128)S(1)}, s32[128]{0:T(128)}, u32[]{:S(2)}) copy-start(s32[128]{0:T(128)} %get-tuple-element.47) | copy-start | bytes 1540
  68.4 6.2 %copy-start.8 = (s32[128]{0:T(128)S(1)}, s32[128]{0:T(128)}, u32[]{:S(2)}) copy-start(s32[128]{0:T(128)} %get-tuple-element.44) | copy-start | bytes 1540
  68.4 6.2 %copy-start.9 = (s32[128]{0:T(128)S(1)}, s32[128]{0:T(128)}, u32[]{:S(2)}) copy-start(s32[128]{0:T(128)} %get-tuple-element.45) | copy-start | bytes 1540
  68.4 6.2 %copy-start.10 = (s32[128]{0:T(128)S(1)}, s32[128]{0:T(128)}, u32[]{:S(2)}) copy-start(s32[128]{0:T(128)} %get-tuple-element.42) | copy-start | bytes 1540
  68.4 6.2 %copy-start.11 = (s32[128]{0:T(128)S(1)}, s32[128]{0:T(128)}, u32[]{:S(2)}) copy-start(s32[128]{0:T(128)} %get-tuple-element.43) | copy-start | bytes 1540
  68.4 6.2 %copy-start.12 = (s32[128]{0:T(128)S(1)}, s32[128]{0:T(128)}, u32[]{:S(2)}) copy-start(s32[128]{0:T(128)} %get-tuple-element.40) | copy-start | bytes 1540
  68.4 6.2 %copy-start.13 = (s32[128]{0:T(128)S(1)}, s32[128]{0:T(128)}, u32[]{:S(2)}) copy-start(s32[128]{0:T(128)} %get-tuple-element.41) | copy-start | bytes 1540
  72.8 1.1 copy-start.1
  73.8 0.7 copy-start.2
  149.8 1.0 copy-start.3
  149.8 1.1 copy-start.4
  179.9 3.9 %copy-start.5 = (f32[64,64]{1,0:T(8,128)S(1)}, f32[64,64]{1,0:T(8,128)}, u32[]{:S(2)}) copy-start(f32[64,64]{1,0:T(8,128)} %param.12) | copy-start | bytes 49156
Sparse Core Ops, SparseCore 0:
  126.0 22.6 reduce-scatter.3
where the time goes:
time: 234 us; the launch traced here: 233 us
  blocking collectives  63.2 us (27%)
  local copies, waits for them, and re-layouts  61.4 us (26%)
  Pallas kernels  50.5 us (22%)
  waiting for transfers between devices  22.8 us (10%)
  other arithmetic  16.4 us (7%)
  between operations  15.6 us (7%)
  matrix products  2.94 us (1%)
    pallas_call x1, Pallas kernels, window(): pl.pallas_call(window_kernel, out_shape=jax.ShapeDtypeStruct((2,) + field...  46.2 us
    psum x1, blocking collectives, body(): lax.psum((grad_first, grad_second), ('shot', 'gx', 'gy'))  40.3 us
    all_gather x1, blocking collectives, body(): lax.all_gather(jnp.stack([slab_mod, slab_buoy]), 'shot', axis=3, tiled=True)  22.9 us
    unnamed x2, waiting for transfers between devices  22.8 us
    transpose x1, local copies, waits for them, and re-layouts, decoder_grads(): grad_out = grad_fine.reshape(2, size_x // 4, 4, size_y // 4, 4, size_z //...  17 us
    div x4, local copies, waits for them, and re-layouts, materials(): wave_speed = 0.15 + 0.25 * jax.nn.sigmoid(fine_out[0])  14.6 us
    unnamed x38, local copies, waits for them, and re-layouts  13 us
    reshape x2, local copies, waits for them, and re-layouts, decode(): outputs.reshape(depth_c, rows_x, rows_y, 2, 4, 4, 4)  6.48 us
  transfers between devices with their start and end apart: 1, of which 1 were waited for; matrix products, arithmetic and copies ran while one was open for 0% of the time, Pallas kernels for 0%

commit v1 on v0

--- a/solution.py
+++ b/solution.py
@@ -12,53 +12,247 @@
 coeffs = (1225.0 / 1024.0, -245.0 / 3072.0, 49.0 / 5120.0, -5.0 / 7168.0)
 
 
-def decode(latent, w_first, w_second):
-    depth_c, rows_x, merged = latent.shape
-    rows_y = merged // CH
-    flattened = latent.reshape(-1, CH)
-    hidden = jnp.tanh(jnp.dot(flattened, w_first, precision=lax.Precision.HIGHEST))
-    outputs = jnp.dot(hidden, w_second, precision=lax.Precision.HIGHEST)
-    fine_out = (
-        outputs.reshape(depth_c, rows_x, rows_y, 2, 4, 4, 4)
-        .transpose(3, 1, 4, 2, 5, 0, 6)
-        .reshape(2, rows_x * 4, rows_y * 4, depth_c * 4)
-    )
-    return (flattened, hidden, fine_out)
-
-
-def materials(fine_out):
-    wave_speed = 0.15 + 0.25 * jax.nn.sigmoid(fine_out[0])
-    density = 1.0 + 1.5 * jax.nn.sigmoid(fine_out[1])
-    return (density * wave_speed * wave_speed, 1.0 / density)
-
-
-def decoder_grads(flattened, hidden, fine_out, grad_mod, grad_buoy, w_first, w_second):
-    sig_speed = jax.nn.sigmoid(fine_out[0])
-    sig_dens = jax.nn.sigmoid(fine_out[1])
-    wave_speed = 0.15 + 0.25 * sig_speed
-    density = 1.0 + 1.5 * sig_dens
-    grad_speed = grad_mod * 2.0 * density * wave_speed
-    grad_dens = grad_mod * wave_speed * wave_speed - grad_buoy / (density * density)
-    grad_fine = jnp.stack(
-        [
-            grad_speed * 0.25 * sig_speed * (1.0 - sig_speed),
-            grad_dens * 1.5 * sig_dens * (1.0 - sig_dens),
+def axis_peers(axis, distance):
+    count = lax.axis_size(axis)
+    return {axis: lax.rem(lax.axis_index(axis) + distance, count)}
+
+
+def greet(axes):
+    barrier = pltpu.get_barrier_semaphore()
+    total = 0
+    for axis in axes:
+        for distance in range(1, lax.axis_size(axis)):
+            pl.semaphore_signal(
+                barrier,
+                inc=1,
+                device_id=axis_peers(axis, distance),
+                device_id_type=pl.DeviceIdType.MESH,
+            )
+            total += 1
+    pl.semaphore_wait(barrier, total)
+
+
+def to_peer(axis, distance, source, dest, sems, row):
+    return pltpu.make_async_remote_copy(
+        src_ref=source,
+        dst_ref=dest,
+        send_sem=sems.at[0, row, distance - 1],
+        recv_sem=sems.at[1, row, distance - 1],
+        device_id=axis_peers(axis, distance),
+        device_id_type=pl.DeviceIdType.MESH,
+    )
+
+
+def gather_kernel(own_ref, out_ref, sems):
+    greet(("shot",))
+    me = lax.axis_index("shot")
+    copies = [
+        to_peer("shot", d, own_ref, out_ref.at[me], sems, 0)
+        for d in range(1, lax.axis_size("shot"))
+    ]
+    for copy in copies:
+        copy.start()
+    out_ref[me] = own_ref[...]
+    for copy in copies:
+        copy.wait()
+
+
+def gather_latent(own):
+    shots = lax.axis_size("shot")
+    vmem = pl.BlockSpec(memory_space=pltpu.VMEM)
+    return pl.pallas_call(
+        gather_kernel,
+        out_shape=jax.ShapeDtypeStruct((shots,) + own.shape, jnp.float32),
+        in_specs=[vmem],
+        out_specs=vmem,
+        scratch_shapes=[pltpu.SemaphoreType.DMA((2, 1, shots - 1))],
+        compiler_params=pltpu.CompilerParams(collective_id=1, has_side_effects=True),
+    )(own)
+
+
+def reduce_kernel(share_ref, weight_ref, out_ref, sum_ref, landed, first, second, third, sems):
+    greet(("shot", "gx", "gy"))
+    me = lax.axis_index("shot")
+    copies = []
+    for d in range(1, lax.axis_size("shot")):
+        there = axis_peers("shot", d)["shot"]
+        copies.append(to_peer("shot", d, weight_ref, first.at[me], sems, 0))
+        copies.append(to_peer("shot", d, share_ref.at[there], landed.at[me], sems, 1))
+    for copy in copies:
+        copy.start()
+    first[me] = weight_ref[...]
+    landed[me] = share_ref[me]
+
+    def total(stack):
+        summed = stack[0]
+        for n in range(1, stack.shape[0]):
+            summed = summed + stack[n]
+        return summed
+
+    for copy in copies[::2]:
+        copy.wait()
+    held, slots, row = first, second, 2
+    for axis in ("gx", "gy"):
+        mine = lax.axis_index(axis)
+        slots[mine] = total(held)
+        hops = [
+            to_peer(axis, d, slots.at[mine], slots.at[mine], sems, row)
+            for d in range(1, lax.axis_size(axis))
         ]
-    )
-    size_x, size_y, size_z = (grad_fine.shape[1], grad_fine.shape[2], grad_fine.shape[3])
-    grad_out = (
-        grad_fine.reshape(2, size_x // 4, 4, size_y // 4, 4, size_z // 4, 4)
-        .transpose(5, 1, 3, 0, 2, 4, 6)
-        .reshape(-1, 128)
-    )
-    grad_hidden = jnp.dot(grad_out, w_second.T, precision=lax.Precision.HIGHEST)
-    grad_pre = grad_hidden * (1.0 - hidden * hidden)
-    grad_latent = jnp.dot(grad_pre, w_first.T, precision=lax.Precision.HIGHEST).reshape(
-        size_z // 4, size_x // 4, size_y // 4 * CH
-    )
-    grad_second = jnp.dot(hidden.T, grad_out, precision=lax.Precision.HIGHEST)
-    grad_first = jnp.dot(flattened.T, grad_pre, precision=lax.Precision.HIGHEST)
-    return (grad_latent, grad_first, grad_second)
+        for hop in hops:
+            hop.start()
+        if axis == "gx":
+            for copy in copies[1::2]:
+                copy.wait()
+            out_ref[...] = total(landed)
+        for hop in hops:
+            hop.wait()
+        held, slots, row = slots, third, row + 1
+    sum_ref[...] = total(held)
+
+
+def reduce_all(shares, weights):
+    sizes = [lax.axis_size(axis) for axis in ("shot", "gx", "gy")]
+    vmem = pl.BlockSpec(memory_space=pltpu.VMEM)
+    return pl.pallas_call(
+        reduce_kernel,
+        out_shape=(
+            jax.ShapeDtypeStruct(shares.shape[1:], jnp.float32),
+            jax.ShapeDtypeStruct(weights.shape, jnp.float32),
+        ),
+        in_specs=[vmem, vmem],
+        out_specs=(vmem, vmem),
+        scratch_shapes=[pltpu.VMEM(shares.shape, jnp.float32)]
+        + [pltpu.VMEM((size,) + weights.shape, jnp.float32) for size in sizes]
+        + [pltpu.SemaphoreType.DMA((2, 4, max(sizes)))],
+        compiler_params=pltpu.CompilerParams(collective_id=2, has_side_effects=True),
+    )(shares, weights)
+
+
+exact = lax.Precision.HIGHEST
+contract_lanes = (((1,), (1,)), ((), ()))
+
+
+def by_offset(values_in):
+    offset = lax.broadcasted_iota(jnp.int32, values_in.shape, 1) % 4
+    return [jnp.where(offset == k, values_in, 0.0) for k in range(4)]
+
+
+def decode_kernel(wide_ref, first_ref, second_ref, mod_ref, buoy_ref, hidden_ref, fine_ref):
+    rows_b, size_z = wide_ref.shape[1], wide_ref.shape[3]
+
+    def row(a, carry):
+        latent = jnp.concatenate([wide_ref[a, b] for b in range(rows_b)], axis=1)
+        hidden = jnp.tanh(jnp.dot(first_ref[...], latent, precision=exact))
+        hidden_ref[a] = hidden
+        fine = jnp.dot(
+            second_ref[...], jnp.concatenate(by_offset(hidden), axis=0), precision=exact
+        )
+        fine_ref[a] = fine
+        speed = 0.15 + 0.25 * jax.nn.sigmoid(fine[:16])
+        density = 1.0 + 1.5 * jax.nn.sigmoid(fine[16:])
+        modulus = density * speed * speed
+        buoyancy = 1.0 / density
+        for i in range(4):
+            for b in range(rows_b):
+                lanes = slice(b * size_z, (b + 1) * size_z)
+                mod_ref[4 * a + i, 4 * b : 4 * b + 4] = modulus[4 * i : 4 * i + 4, lanes]
+                buoy_ref[4 * a + i, 4 * b : 4 * b + 4] = buoyancy[4 * i : 4 * i + 4, lanes]
+        return carry
+
+    lax.fori_loop(0, wide_ref.shape[0], row, 0)
+
+
+def decode(wide, w_first, w_second):
+    rows_a, rows_b, channels, size_z = wide.shape
+    field = jax.ShapeDtypeStruct((4 * rows_a, 4 * rows_b, size_z), jnp.float32)
+    lanes = rows_b * size_z
+    by_k = w_second.reshape(channels, 32, 4).transpose(1, 2, 0).reshape(32, 4 * channels)
+    return pl.pallas_call(
+        decode_kernel,
+        out_shape=(
+            field,
+            field,
+            jax.ShapeDtypeStruct((rows_a, channels, lanes), jnp.float32),
+            jax.ShapeDtypeStruct((rows_a, 32, lanes), jnp.float32),
+        ),
+        compiler_params=pltpu.CompilerParams(vmem_limit_bytes=40 * 1024 * 1024),
+    )(wide, w_first.T, by_k)
+
+
+def gradient_kernel(
+    totals_ref, wide_ref, hidden_ref, fine_ref, first_ref, back_ref, out_ref, gf_ref, gs_ref, mix
+):
+    rows_b, size_z = wide_ref.shape[1], wide_ref.shape[3]
+    gf_ref[...] = jnp.zeros(gf_ref.shape, jnp.float32)
+    gs_ref[...] = jnp.zeros(gs_ref.shape, jnp.float32)
+
+    def row(a, carry):
+        for field in range(2):
+            for i in range(4):
+                for b in range(rows_b):
+                    top = 16 * field + 4 * i
+                    mix[top : top + 4, b * size_z : (b + 1) * size_z] = totals_ref[
+                        field, 4 * a + i, 4 * b : 4 * b + 4
+                    ]
+        grad_mod, grad_buoy = mix[:16], mix[16:]
+        sig_speed = jax.nn.sigmoid(fine_ref[a, :16])
+        sig_dens = jax.nn.sigmoid(fine_ref[a, 16:])
+        speed = 0.15 + 0.25 * sig_speed
+        density = 1.0 + 1.5 * sig_dens
+        grad_speed = grad_mod * 2.0 * density * speed
+        grad_dens = grad_mod * speed * speed - grad_buoy / (density * density)
+        grad_fine = jnp.concatenate(
+            [
+                grad_speed * 0.25 * sig_speed * (1.0 - sig_speed),
+                grad_dens * 1.5 * sig_dens * (1.0 - sig_dens),
+            ],
+            axis=0,
+        )
+        hidden = hidden_ref[a]
+        channels = hidden.shape[0]
+        spread = jnp.dot(back_ref[...], grad_fine, precision=exact)
+        offset = lax.broadcasted_iota(jnp.int32, hidden.shape, 1) % 4
+        grad_hidden = 0.0
+        for k in range(4):
+            grad_hidden = grad_hidden + jnp.where(
+                offset == k, spread[k * channels : (k + 1) * channels], 0.0
+            )
+        grad_pre = grad_hidden * (1.0 - hidden * hidden)
+        grad_wide = jnp.dot(first_ref[...], grad_pre, precision=exact)
+        for b in range(rows_b):
+            out_ref[a, b] = grad_wide[:, b * size_z : (b + 1) * size_z]
+        latent = jnp.concatenate([wide_ref[a, b] for b in range(rows_b)], axis=1)
+        gf_ref[...] += lax.dot_general(
+            latent, grad_pre, contract_lanes, precision=exact, preferred_element_type=jnp.float32
+        )
+        gs_ref[...] += lax.dot_general(
+            jnp.concatenate(by_offset(hidden), axis=0),
+            grad_fine,
+            contract_lanes,
+            precision=exact,
+            preferred_element_type=jnp.float32,
+        )
+        return carry
+
+    lax.fori_loop(0, wide_ref.shape[0], row, 0)
+
+
+def decoder_grads(totals, wide, hidden, fine, w_first, w_second):
+    rows_a, rows_b, channels, size_z = wide.shape
+    back = w_second.reshape(channels, 32, 4).transpose(2, 0, 1).reshape(4 * channels, 32)
+    grad_wide, grad_first, by_k = pl.pallas_call(
+        gradient_kernel,
+        out_shape=(
+            jax.ShapeDtypeStruct(wide.shape, jnp.float32),
+            jax.ShapeDtypeStruct((channels, channels), jnp.float32),
+            jax.ShapeDtypeStruct((4 * channels, 32), jnp.float32),
+        ),
+        scratch_shapes=[pltpu.VMEM((32, rows_b * size_z), jnp.float32)],
+        compiler_params=pltpu.CompilerParams(vmem_limit_bytes=40 * 1024 * 1024),
+    )(totals, wide, hidden, fine, w_first, back)
+    grad_second = by_k.reshape(4, channels, 32).transpose(1, 2, 0).reshape(channels, 128)
+    return grad_wide, grad_first, grad_second
 
 
 RIM = 7
@@ -317,8 +511,6 @@
         & (lax.broadcasted_iota(jnp.int32, (size_y, size_z), 1) == src_z)
     ).astype(jnp.float32)
     chunk = 8 if size_x % 8 == 0 else 1
-    exact = lax.Precision.HIGHEST
-
     def step(state, way, moment):
         def depth_part(turn, carry):
             here = pl.ds(turn * chunk, chunk)
@@ -504,10 +696,21 @@
     size_x, size_y = (fwd_press.shape[1], fwd_press.shape[2])
     anchor_x = lax.axis_index("gx") * size_x
     anchor_y = lax.axis_index("gy") * size_y
-    flattened, hidden, fine_out = decode(latent, w_first, w_second)
-    slab_mod, slab_buoy = materials(fine_out)
-    stacked = lax.all_gather(jnp.stack([slab_mod, slab_buoy]), "shot", axis=3, tiled=True)
-    modulus, buoyancy = (stacked[0], stacked[1])
+    depth_c, rows_x, merged = latent.shape
+    size_z = fwd_press.shape[3]
+    everything = gather_latent(latent.reshape(depth_c, rows_x * merged))
+    all_depth = size_z // 4
+    repeat = (
+        lax.broadcasted_iota(jnp.int32, (all_depth, size_z), 1) // 4
+        == lax.broadcasted_iota(jnp.int32, (all_depth, size_z), 0)
+    ).astype(jnp.float32)
+    wide = lax.dot_general(
+        everything.reshape(all_depth, rows_x * merged),
+        repeat,
+        (((0,), (0,)), ((), ())),
+        precision=exact,
+    ).reshape(rows_x, merged // CH, CH, size_z)
+    modulus, buoyancy, hidden, fine = decode(wide, w_first, w_second)
     hits, recorded = receiver_fields(
         rec_pos[0], observed[0], anchor_x, anchor_y, fwd_press.shape[1:]
     )
@@ -524,12 +727,17 @@
         hits,
         recorded,
     )
-    shares = lax.psum_scatter(totals, "shot", scatter_dimension=3, tiled=True)
-    grad_latent, grad_first, grad_second = decoder_grads(
-        flattened, hidden, fine_out, shares[0], shares[1], w_first, w_second
-    )
-    grad_first, grad_second = lax.psum((grad_first, grad_second), ("shot", "gx", "gy"))
-    return (grad_latent, grad_first, grad_second)
+    grad_wide, grad_first, grad_second = decoder_grads(
+        totals, wide, hidden, fine, w_first, w_second
+    )
+    grad_depth = lax.dot_general(
+        repeat, grad_wide.reshape(rows_x * merged, size_z), contract_lanes, precision=exact
+    )
+    weights = jnp.concatenate(
+        [grad_second, jnp.pad(grad_first, ((0, 0), (0, 128 - CH)))], axis=0
+    )
+    own, weights = reduce_all(grad_depth.reshape(-1, depth_c, rows_x * merged), weights)
+    return (own.reshape(latent.shape), weights[CH:, :CH], weights[:CH])
 
 
 def solution(mesh):

time: 234 us -> 125 us (0.53)
  blocking collectives: 63.2 us -> 0 us
  Pallas kernels: 50.5 us -> 99.1 us
  local copies, waits for them, and re-layouts: 61.4 us -> 15.2 us
  waiting for transfers between devices: 22.8 us -> 0 us
  between operations: 15.6 us -> 2.11 us
  other arithmetic: 16.4 us -> 4.25 us
    pallas_call x0 -> x4, Pallas kernels: none -> 48.5 us  [the longest x1 19.3 us: reduce_all(): pl.pallas_call(reduce_kernel, out_shape=(jax.ShapeDtypeStruct(shares.shap...]
    psum x1 -> x0, blocking collectives: 40.3 us -> none  [body(): lax.psum((grad_first, grad_second), ('shot', 'gx', 'gy'))]
    all_gather x1 -> x0, blocking collectives: 22.9 us -> none  [body(): lax.all_gather(jnp.stack([slab_mod, slab_buoy]), 'shot', axis=3, tiled=True)]
    unnamed x2 -> x0, waiting for transfers between devices: 22.8 us -> none
    transpose x1, local copies, waits for them, and re-layouts: 17 us -> 0.09 us  [decoder_grads(): w_second.reshape(channels, 32, 4).transpose(2, 0, 1)]
    div x4 -> x0, local copies, waits for them, and re-layouts: 14.6 us -> none  [materials(): wave_speed = 0.15 + 0.25 * jax.nn.sigmoid(fine_out[0])]
    reshape x5 -> x3, local copies, waits for them, and re-layouts: 9.63 us -> 0.26 us  [the longest x2 0.16 us: decoder_grads(): by_k.reshape(4, channels, 32).transpose(1, 2, 0).reshape(channels, 128)]
    transpose x1 -> x0, other arithmetic: 5.67 us -> none  [decoder_grads(): grad_out = grad_fine.reshape(2, size_x // 4, 4, size_y // 4, 4, size_z //...]
  transfers between devices with their start and end apart: 1 -> 0, of which waited for: 1 -> 0; matrix products, arithmetic and copies ran while one was open for 0% -> 0% of each run, Pallas kernels for 0% -> 0%
where the time goes in v1:
time: 125 us; the launch traced here: 124 us
  Pallas kernels  99.1 us (79%)
  local copies, waits for them, and re-layouts  15.2 us (12%)
  other arithmetic  4.25 us (3%)
  matrix products  3.54 us (3%)
  between operations  2.11 us (2%)
    pallas_call x1, Pallas kernels, window(): pl.pallas_call(window_kernel, out_shape=jax.ShapeDtypeStruct((2,) + field...  46.3 us
    pallas_call x1, Pallas kernels, reduce_all(): pl.pallas_call(reduce_kernel, out_shape=(jax.ShapeDtypeStruct(shares.shap...  19.3 us
    pallas_call x1, Pallas kernels, decoder_grads(): pl.pallas_call(gradient_kernel, out_shape=(jax.ShapeDtypeStruct(wide.shap...  13.8 us
    unnamed x27, local copies, waits for them, and re-layouts  11 us
    pallas_call x1, Pallas kernels, gather_latent(): pl.pallas_call(gather_kernel, out_shape=jax.ShapeDtypeStruct((shots,) + o...  9.43 us
    pallas_call x1, Pallas kernels, decode(): pl.pallas_call(decode_kernel, out_shape=(field, field, jax.ShapeDtypeStru...  5.85 us
    pallas_call x1, Pallas kernels, receiver_fields(): pl.pallas_call(receiver_kernel, out_shape=(jax.ShapeDtypeStruct(shape, jn...  4.3 us
    slice x2, local copies, waits for them, and re-layouts, body(): return (own.reshape(latent.shape), weights[CH:, :CH], weights[:CH])  2.75 us

profile of v1, /device:TPU:0, one launch (start us, length us, event | category | flops | bytes accessed | tf_op | source)
XLA Modules:
  0.0 124.2 jit_solution(9681224550513713652)
XLA Ops:
  0.6 0.8 slice_bitcast_fusion
  1.4 0.8 bitcast_reduce-precision_fusion
  2.3 4.3 %shard_map.132 = (f32[24,32,128]{2,1,0:T(8,128)S(1)}, f32[3,24,32,128]{3,2,1,0:T(8,128)S(1)}) custom-call(s32[1,2048]{1,0:T(1,128)S(1)} %get-tuple-element.28.column_ref, s32[1,2048]{1,0:T(1,128)S(1)} %get-tuple-element.27.depth_ref, f32[6,2048]{1,0:T(8,128)S(1)} %reshape.174.parts_ref), custom_call_target="tpu_custom_call" | custom-call | flops 2818572288 | bytes 1572864 | tf_op jit(solution)/shard_map/pallas_call | solution.py:306
  6.6 1.0 copy-done.3
  7.6 0.8 copy-done.6
  8.4 9.4 %shard_map.130 = f32[4,8,3072]{2,1,0:T(8,128)} custom-call(f32[8,3072]{1,0:T(8,128)} %bitcast.58), custom_call_target="tpu_custom_call" | custom-call | tf_op jit(solution)/shard_map/pallas_call | solution.py:63
  17.8 1.8 %convolution_bitcast_fusion = f32[3072,128]{0,1:T(8,128)S(1)} fusion(f32[4,8,3072]{2,1,0:T(8,128)} %shard_map.130, s32[128]{0:T(128)S(1)} %get-tuple-element.42, s32[128]{0:T(128)S(1)} %get-tuple-element.43, pred[128]{0:T(512)(128)(4,1)S(1)} %compare_and_fusion), kind=kOutput, calls=%fused_computation | convolution fusion | flops 151003136 | bytes 1967232 | tf_op jit(solution)/shard_map/dot_general | solution.py:707
  19.7 0.5 copy.19
  20.2 0.3 copy-done.10
  20.4 0.1 copy.21
  20.5 0.1 reshape.173.second_ref
  20.7 5.8 %shard_map.131 = (f32[24,32,128]{2,1,0:T(8,128)S(1)}, f32[24,32,128]{2,1,0:T(8,128)S(1)}, f32[6,64,1024]{2,1,0:T(8,128)S(1)}, f32[6,32,1024]{2,1,0:T(8,128)S(1)}) custom-call(f32[6,8,64,128]{3,2,1,0:T(8,128)S(1)} %bitcast.44, f32[64,64]{1,0:T(8,128)S(1)} %bitcast.48, f32[32,256]{1,0:T(8,128)S(1)} %reshape.173.second_ref), custom_call_target="tpu_custom_call" | custom-call | tf_op jit(solution)/shard_map/pallas_call | solution.py:171
  26.6 1.1 copy-done.1
  27.7 0.9 copy-done.4
  28.6 0.8 copy-done.7
  29.4 0.8 copy-done.8
  30.1 0.6 fusion.35
  32.0 1.2 %pad_add_fusion.place_ref = s32[3]{0:T(128)} fusion(s32[1]{0:T(128)} %bitcast.4, s32[1]{0:T(128)} %bitcast.3, s32[1]{0:T(128)} %bitcast.1), kind=kLoop, calls=%fused_computation.68 | loop fusion | flops 6 | bytes 24 | tf_op jit(solution)/shard_map/stack | solution.py:717
  33.3 0.7 fusion.16
  34.0 46.3 %shard_map.133.totals_ref = f32[2,24,32,128]{3,2,1,0:T(8,128)} custom-call(s32[3]{0:T(128)} %pad_add_fusion.place_ref, f32[3]{0:T(128)} %bitcast.59, f32[128,128]{1,0:T(8,128)} %get-tuple-element.30.dplus_ref, f32[128,128]{1,0:T(8,128)} %get-tuple-element.29.dminus_ref, f32[24,32,128]{2,1,0:T(8,128)} %copy-done.7, f32[24,32,128]{2,1,0:T(8,128)} %copy-done.8, ...), custom_call_target="tpu_custom_call" | custom-call | tf_op jit(solution)/shard_map/pallas_call | solution.py:656
  80.3 0.1 copy.22
  80.5 1.1 copy-done
  81.6 1.4 %copy-done.2 = f32[6,64,1024]{2,1,0:T(8,128)S(1)} copy-done((f32[6,64,1024]{2,1,0:T(8,128)S(1)}, f32[6,64,1024]{2,1,0:T(8,128)}, u32[]{:S(2)}) %copy-start.2) | copy-done | bytes 1572888
  83.0 1.1 copy-done.5
  84.1 13.8 %shard_map.134 = (f32[6,8,64,128]{3,2,1,0:T(8,128)S(1)}, f32[64,64]{1,0:T(8,128)S(1)}, f32[256,32]{1,0:T(8,128)S(1)}) custom-call(f32[2,24,32,128]{3,2,1,0:T(8,128)S(1)} %copy-done, f32[6,8,64,128]{3,2,1,0:T(8,128)S(1)} %bitcast.45, f32[6,64,1024]{2,1,0:T(8,128)S(1)} %copy-done.2, f32[6,32,1024]{2,1,0:T(8,128)S(1)} %copy-done.5, f32[64,64]{1,0:T(8,128)S(1)} %copy-done.9, ...), custom_call_target="tpu_custom_call" | custom-call | tf_op jit(solution)/shard_map/pallas_call | solution.py:244
  98.0 0.1 copy.23
  98.1 0.7 select_maximum_fusion.weight_ref
  98.8 1.7 %fusion.26.share_ref = f32[4,8,3072]{2,1,0:T(8,128)} fusion(f32[3072,128,1]{1,0,2:T(8,128)S(1)} %bitcast.46, s32[4,8]{1,0:T(4,128)S(1)} %multiply_add_fusion, s32[128]{0:T(128)S(1)} %get-tuple-element.42, s32[128]{0:T(128)S(1)} %get-tuple-element.43, pred[128]{0:T(512)(128)(4,1)S(1)} %compare_and_fusion), kind=kOutput, calls=%fused_computation.46 | convolution fusion | flops 151003136 | bytes 1967360 | tf_op jit(solution)/shard_map/dot_general | solution.py:733
  100.5 19.3 %shard_map.135 = (f32[8,3072]{1,0:T(8,128)}, f32[128,128]{1,0:T(8,128)}) custom-call(f32[4,8,3072]{2,1,0:T(8,128)} %fusion.26.share_ref, f32[128,128]{1,0:T(8,128)} %select_maximum_fusion.weight_ref), custom_call_target="tpu_custom_call" | custom-call | tf_op jit(solution)/shard_map/pallas_call | solution.py:117
  119.9 1.4 %slice.36 = f32[64,64]{1,0:T(8,128)} slice(f32[128,128]{1,0:T(8,128)} %get-tuple-element.24), slice={[64:128], [0:64]} | slice | bytes 32768 | tf_op jit(solution)/shard_map/slice | solution.py:740
  121.3 1.4 %slice.37 = f32[64,128]{1,0:T(8,128)} slice(f32[128,128]{1,0:T(8,128)} %get-tuple-element.24), slice={[0:64], [0:128]} | slice | bytes 65536 | tf_op jit(solution)/shard_map/slice | solution.py:740
  122.6 1.5 %copy.26 = f32[8,6,512]{2,0,1:T(8,128)} copy(f32[8,6,512]{2,0,1:T(8,128)} %bitcast.57) | data formatting | bytes 196608
  (25 shorter events, 0.3 us)
Async XLA Ops:
  6.6 1.0 copy-start.3
  7.6 0.8 copy-start.6
  19.7 0.8 copy-start.10
  19.7 1.0 copy-start.9
  20.1 10.0 %copy-start.11 = (s32[3,1]{0,1:T(1,128)S(1)}, s32[3,1]{0,1:T(1,128)}, u32[]{:S(2)}) copy-start(s32[3,1]{0,1:T(1,128)} %param.18) | copy-start | bytes 40
  26.6 1.2 copy-start.1
  27.7 0.9 copy-start.4
  28.6 0.8 copy-start.7
  29.4 0.8 copy-start.8
  80.4 1.1 copy-start
  81.6 1.4 %copy-start.2 = (f32[6,64,1024]{2,1,0:T(8,128)S(1)}, f32[6,64,1024]{2,1,0:T(8,128)}, u32[]{:S(2)}) copy-start(f32[6,64,1024]{2,1,0:T(8,128)} %copy-done.1) | copy-start | bytes 4718596
  83.0 1.1 copy-start.5

commit v2 on v1

--- a/solution.py
+++ b/solution.py
@@ -78,7 +78,7 @@
         there = axis_peers("shot", d)["shot"]
         copies.append(to_peer("shot", d, weight_ref, first.at[me], sems, 0))
         copies.append(to_peer("shot", d, share_ref.at[there], landed.at[me], sems, 1))
-    for copy in copies:
+    for copy in copies[::2] + copies[1::2]:
         copy.start()
     first[me] = weight_ref[...]
     landed[me] = share_ref[me]
@@ -568,7 +568,7 @@
 
         lax.fori_loop(0, VRIM, ghost_low, 0)
         lax.fori_loop(size_x + VRIM, size_x + 2 * VRIM - 1, ghost_low, 0)
-        lax.fori_loop(0, size_x, faces, 0)
+        lax.fori_loop(0, size_x, faces, 0, unroll=2)
 
         def finish(k, carry):
             x = lax.rem(k + size_x - RIM, size_x)
@@ -611,11 +611,11 @@
             return carry
 
         edge = min(2 * RIM, size_x)
-        lax.fori_loop(0, edge, finish, 0)
+        lax.fori_loop(0, edge, finish, 0, unroll=2)
         more = state + 1 < 2 * STEPS
         if more:
             send(state + 1, (0, 1))
-        lax.fori_loop(edge, size_x, finish, 0)
+        lax.fori_loop(edge, size_x, finish, 0, unroll=2)
         if more:
             send(state + 1, (2, 3))
 

time: 125 us -> 121 us (0.968)
  Pallas kernels: 99.1 us -> 95.2 us
    pallas_call x1, Pallas kernels: 19.3 us -> 16.8 us  [reduce_all(): pl.pallas_call(reduce_kernel, out_shape=(jax.ShapeDtypeStruct(shares.shap...]
where the time goes in v2:
time: 121 us; the launch traced here: 120 us
  Pallas kernels  95.2 us (79%)
  local copies, waits for them, and re-layouts  15.2 us (13%)
  other arithmetic  4.25 us (4%)
  matrix products  3.54 us (3%)
  between operations  2.11 us (2%)
    pallas_call x1, Pallas kernels, window(): pl.pallas_call(window_kernel, out_shape=jax.ShapeDtypeStruct((2,) + field...  45.1 us
    pallas_call x1, Pallas kernels, reduce_all(): pl.pallas_call(reduce_kernel, out_shape=(jax.ShapeDtypeStruct(shares.shap...  16.8 us
    pallas_call x1, Pallas kernels, decoder_grads(): pl.pallas_call(gradient_kernel, out_shape=(jax.ShapeDtypeStruct(wide.shap...  13.8 us
    unnamed x27, local copies, waits for them, and re-layouts  11 us
    pallas_call x1, Pallas kernels, gather_latent(): pl.pallas_call(gather_kernel, out_shape=jax.ShapeDtypeStruct((shots,) + o...  9.44 us
    pallas_call x1, Pallas kernels, decode(): pl.pallas_call(decode_kernel, out_shape=(field, field, jax.ShapeDtypeStru...  5.85 us
    pallas_call x1, Pallas kernels, receiver_fields(): pl.pallas_call(receiver_kernel, out_shape=(jax.ShapeDtypeStruct(shape, jn...  4.3 us
    slice x2, local copies, waits for them, and re-layouts, body(): return (own.reshape(latent.shape), weights[CH:, :CH], weights[:CH])  2.75 us

profile of v2, /device:TPU:0, one launch (start us, length us, event | category | flops | bytes accessed | tf_op | source)
XLA Modules:
  0.0 120.3 jit_solution(11928300076057921796)
XLA Ops:
  0.6 0.8 slice_bitcast_fusion
  1.4 0.8 bitcast_reduce-precision_fusion
  2.3 4.3 %shard_map.132 = (f32[24,32,128]{2,1,0:T(8,128)S(1)}, f32[3,24,32,128]{3,2,1,0:T(8,128)S(1)}) custom-call(s32[1,2048]{1,0:T(1,128)S(1)} %get-tuple-element.28.column_ref, s32[1,2048]{1,0:T(1,128)S(1)} %get-tuple-element.27.depth_ref, f32[6,2048]{1,0:T(8,128)S(1)} %reshape.174.parts_ref), custom_call_target="tpu_custom_call" | custom-call | flops 2818572288 | bytes 1572864 | tf_op jit(solution)/shard_map/pallas_call | solution.py:306
  6.6 1.0 copy-done.3
  7.6 0.8 copy-done.6
  8.4 9.4 %shard_map.130 = f32[4,8,3072]{2,1,0:T(8,128)} custom-call(f32[8,3072]{1,0:T(8,128)} %bitcast.58), custom_call_target="tpu_custom_call" | custom-call | tf_op jit(solution)/shard_map/pallas_call | solution.py:63
  17.8 1.8 %convolution_bitcast_fusion = f32[3072,128]{0,1:T(8,128)S(1)} fusion(f32[4,8,3072]{2,1,0:T(8,128)} %shard_map.130, s32[128]{0:T(128)S(1)} %get-tuple-element.42, s32[128]{0:T(128)S(1)} %get-tuple-element.43, pred[128]{0:T(512)(128)(4,1)S(1)} %compare_and_fusion), kind=kOutput, calls=%fused_computation | convolution fusion | flops 151003136 | bytes 1967232 | tf_op jit(solution)/shard_map/dot_general | solution.py:707
  19.7 0.5 copy.19
  20.2 0.3 copy-done.10
  20.4 0.1 copy.21
  20.5 0.1 reshape.173.second_ref
  20.7 5.8 %shard_map.131 = (f32[24,32,128]{2,1,0:T(8,128)S(1)}, f32[24,32,128]{2,1,0:T(8,128)S(1)}, f32[6,64,1024]{2,1,0:T(8,128)S(1)}, f32[6,32,1024]{2,1,0:T(8,128)S(1)}) custom-call(f32[6,8,64,128]{3,2,1,0:T(8,128)S(1)} %bitcast.44, f32[64,64]{1,0:T(8,128)S(1)} %bitcast.48, f32[32,256]{1,0:T(8,128)S(1)} %reshape.173.second_ref), custom_call_target="tpu_custom_call" | custom-call | tf_op jit(solution)/shard_map/pallas_call | solution.py:171
  26.6 1.1 copy-done.1
  27.7 0.9 copy-done.4
  28.6 0.8 copy-done.7
  29.4 0.8 copy-done.8
  30.2 0.6 fusion.35
  32.0 1.2 %pad_add_fusion.place_ref = s32[3]{0:T(128)} fusion(s32[1]{0:T(128)} %bitcast.4, s32[1]{0:T(128)} %bitcast.3, s32[1]{0:T(128)} %bitcast.1), kind=kLoop, calls=%fused_computation.68 | loop fusion | flops 6 | bytes 24 | tf_op jit(solution)/shard_map/stack | solution.py:717
  33.3 0.7 fusion.16
  34.0 45.1 %shard_map.133.totals_ref = f32[2,24,32,128]{3,2,1,0:T(8,128)} custom-call(s32[3]{0:T(128)} %pad_add_fusion.place_ref, f32[3]{0:T(128)} %bitcast.59, f32[128,128]{1,0:T(8,128)} %get-tuple-element.30.dplus_ref, f32[128,128]{1,0:T(8,128)} %get-tuple-element.29.dminus_ref, f32[24,32,128]{2,1,0:T(8,128)} %copy-done.7, f32[24,32,128]{2,1,0:T(8,128)} %copy-done.8, ...), custom_call_target="tpu_custom_call" | custom-call | tf_op jit(solution)/shard_map/pallas_call | solution.py:656
  79.1 0.1 copy.22
  79.2 1.1 copy-done
  80.3 1.4 %copy-done.2 = f32[6,64,1024]{2,1,0:T(8,128)S(1)} copy-done((f32[6,64,1024]{2,1,0:T(8,128)S(1)}, f32[6,64,1024]{2,1,0:T(8,128)}, u32[]{:S(2)}) %copy-start.2) | copy-done | bytes 1572888
  81.8 1.1 copy-done.5
  82.9 13.8 %shard_map.134 = (f32[6,8,64,128]{3,2,1,0:T(8,128)S(1)}, f32[64,64]{1,0:T(8,128)S(1)}, f32[256,32]{1,0:T(8,128)S(1)}) custom-call(f32[2,24,32,128]{3,2,1,0:T(8,128)S(1)} %copy-done, f32[6,8,64,128]{3,2,1,0:T(8,128)S(1)} %bitcast.45, f32[6,64,1024]{2,1,0:T(8,128)S(1)} %copy-done.2, f32[6,32,1024]{2,1,0:T(8,128)S(1)} %copy-done.5, f32[64,64]{1,0:T(8,128)S(1)} %copy-done.9, ...), custom_call_target="tpu_custom_call" | custom-call | tf_op jit(solution)/shard_map/pallas_call | solution.py:244
  96.7 0.1 copy.23
  96.9 0.7 select_maximum_fusion.weight_ref
  97.6 1.7 %fusion.26.share_ref = f32[4,8,3072]{2,1,0:T(8,128)} fusion(f32[3072,128,1]{1,0,2:T(8,128)S(1)} %bitcast.46, s32[4,8]{1,0:T(4,128)S(1)} %multiply_add_fusion, s32[128]{0:T(128)S(1)} %get-tuple-element.42, s32[128]{0:T(128)S(1)} %get-tuple-element.43, pred[128]{0:T(512)(128)(4,1)S(1)} %compare_and_fusion), kind=kOutput, calls=%fused_computation.46 | convolution fusion | flops 151003136 | bytes 1967360 | tf_op jit(solution)/shard_map/dot_general | solution.py:733
  99.3 16.8 %shard_map.135 = (f32[8,3072]{1,0:T(8,128)}, f32[128,128]{1,0:T(8,128)}) custom-call(f32[4,8,3072]{2,1,0:T(8,128)} %fusion.26.share_ref, f32[128,128]{1,0:T(8,128)} %select_maximum_fusion.weight_ref), custom_call_target="tpu_custom_call" | custom-call | tf_op jit(solution)/shard_map/pallas_call | solution.py:117
  116.0 1.4 %slice.36 = f32[64,64]{1,0:T(8,128)} slice(f32[128,128]{1,0:T(8,128)} %get-tuple-element.24), slice={[64:128], [0:64]} | slice | bytes 32768 | tf_op jit(solution)/shard_map/slice | solution.py:740
  117.4 1.4 %slice.37 = f32[64,128]{1,0:T(8,128)} slice(f32[128,128]{1,0:T(8,128)} %get-tuple-element.24), slice={[0:64], [0:128]} | slice | bytes 65536 | tf_op jit(solution)/shard_map/slice | solution.py:740
  118.8 1.5 %copy.26 = f32[8,6,512]{2,0,1:T(8,128)} copy(f32[8,6,512]{2,0,1:T(8,128)} %bitcast.57) | data formatting | bytes 196608
  (25 shorter events, 0.3 us)
Async XLA Ops:
  6.6 1.0 copy-start.3
  7.6 0.8 copy-start.6
  19.7 0.8 copy-start.10
  19.7 1.0 copy-start.9
  20.2 10.0 %copy-start.11 = (s32[3,1]{0,1:T(1,128)S(1)}, s32[3,1]{0,1:T(1,128)}, u32[]{:S(2)}) copy-start(s32[3,1]{0,1:T(1,128)} %param.18) | copy-start | bytes 40
  26.6 1.2 copy-start.1
  27.7 0.9 copy-start.4
  28.6 0.8 copy-start.7
  29.4 0.8 copy-start.8
  79.2 1.1 copy-start
  80.3 1.4 %copy-start.2 = (f32[6,64,1024]{2,1,0:T(8,128)S(1)}, f32[6,64,1024]{2,1,0:T(8,128)}, u32[]{:S(2)}) copy-start(f32[6,64,1024]{2,1,0:T(8,128)} %copy-done.1) | copy-start | bytes 4718596
  81.8 1.1 copy-start.5
